TPU v7x, 32 devices: a whole 2x2x4 slice. The times are simulated.
32 devices in a mesh: rows: 8 (over y, x, core), own: 4 (over z).
Axes of the slice: x: 2, y: 2, z: 4, core: 2. Of those that a mesh axis runs over, the one named last changes fastest.
Arguments:
- emb: bfloat16 [32768, 1024], P(('rows', 'own'))
- send_rows: int32 [32, 8, 256], P(('rows', 'own')), may hold values from 0 to 1024, as said below
- dest_offset: int32 [32, 8, 256], P(('rows', 'own')), may hold values from 0 to 2048, as said below
Outputs:
- centroids: float32 [32, 1024], P('rows')
- dup_score: float32 [32, 2048], P('rows', 'own')
Inputs may be any that keep to these rules, and one draw needn't show every extreme that they name: `send_rows`: each device names each of its 1024 local rows in exactly one slot; the filled slots of a (device, owner) pair come first; for each device a quarter of the owners get all 256 slots filled, a quarter none and the rest 256 / 2. `dest_offset`: filled slots and only they hold a value below 2048. Over all rows that reach one owner from one index of own (exactly 1024 rows), the values are distinct, and cluster c takes the places 0 to n_c - 1, where n_0 to n_3 are 512, 256, 128 and 128 in some order.
All inputs are finite; a program needn't handle non-finite values.
Results may differ from a plain program's by a relative error of at most 0.0039.
Values may be sent and summed in bfloat16 or wider, within the bound.
No kernel may reach another device: no remote copies, remote signals or barrier semaphores. Data moves between devices by JAX's collectives and lax.ppermute only.
A program may use at most 64 MiB of HBM per device.

v0:
```python
import functools
import itertools

import jax
import jax.numpy as jnp
import numpy as np
from jax import lax
from jax.experimental import pallas as pl
from jax.experimental.pallas import tpu as pltpu
from jax.sharding import PartitionSpec as P

KC = 4
EIGHTHS = (4, 4)
CHUNKS = len(EIGHTHS)
SHARPNESS = 20.0
LANES = 128
ROWS = 256
BIG = 56 << 20
SMALL = 16 << 20
UNROLL = 4

vmem = pl.BlockSpec(memory_space=pltpu.VMEM)
smem = pl.BlockSpec(memory_space=pltpu.SMEM)

HOME, MINE, FORWARD, OWN, PAIR, STEP, EXTRA, STEP_FROM, HERE = 0, 4, 5, 6, 7, 8, 9, 10, 11
PLAN_WIDTH = 16

ACROSS = (((1,), (1,)), ((), ()))


def routes(biggest, home, parity):
    step, extra, kinds = {}, {}, []
    for g in range(4):
        to = home[biggest[g]]
        if to == g:
            kinds.append(OWN)
        elif to == g ^ 1:
            kinds.append(PAIR)
        elif to in (1, 2):
            by = 3 - to
            if by not in step:
                step[by] = g
                kinds.append(STEP)
            else:
                if by != 2 - parity:
                    return None
                pair = {step[by], g}
                if pair != {by, by ^ 1}:
                    return None
                step[by] = by ^ 1
                extra[by] = by
                kinds.append(EXTRA)
        else:
            return None
    return step, extra


def build_plans():
    rows = np.zeros((2, 4, 4, 4, 4, 4, PLAN_WIDTH), np.int32)
    for parity in range(2):
        for biggest in itertools.product(range(4), repeat=4):
            best = None
            for home in itertools.permutations(range(4)):
                found = routes(biggest, home, parity)
                if found is not None and (best is None or len(found[1]) < len(best[1][1])):
                    best = (home, found)
            home, (step, extra) = best
            for z in range(4):
                row = rows[(parity,) + biggest][z]
                row[HOME : HOME + 4] = home
                row[MINE] = home.index(z)
                row[FORWARD] = int(z in step and step[z] != z)
                row[OWN] = int(home[biggest[z]] == z)
                row[PAIR] = int(home[biggest[z ^ 1]] == z)
                by = 3 - z
                row[STEP] = int(z in (1, 2) and by in step)
                row[STEP_FROM] = step.get(by, 0) if z in (1, 2) else 0
                row[EXTRA] = int(z in (1, 2) and by in extra)
                row[HERE] = z
    return rows.reshape(-1, PLAN_WIDTH)


PLANS = build_plans()


def pair_table(blocks):
    pairs = [(i, j) for j in range(blocks) for i in range(j + 1)]
    pairs += [(0, 0)] * UNROLL
    return np.asarray(pairs, np.int32).T.copy()


def gather_body(first, ids_ref, emb_ref, out_ref, held, rows_ref, sem, sems):
    groups, per = ids_ref.shape
    local, part = held.shape
    fetch = pltpu.make_async_copy(emb_ref.at[:, first : first + part], held, sem)
    fetch.start()
    columns = jnp.transpose(ids_ref[...])
    lane = lax.broadcasted_iota(jnp.int32, (per, local), 1)
    fetch.wait()
    sends = []
    for o in range(groups):
        at = slice(o * per, (o + 1) * per)
        pick = jnp.where(columns[:, o : o + 1] == lane, 1.0, 0.0).astype(jnp.bfloat16)
        rows = jnp.dot(pick, held[...], preferred_element_type=jnp.float32)
        rows_ref[at, :] = rows.astype(jnp.bfloat16)
        sends.append(pltpu.make_async_copy(rows_ref.at[at], out_ref.at[at], sems.at[o]))
        sends[-1].start()
    for send in sends:
        send.wait()


def gather_rows(ids, emb, first, part):
    slots = ids.size
    local = emb.shape[0]
    groups = ids.shape[0]
    return pl.pallas_call(
        functools.partial(gather_body, first),
        in_specs=[vmem, pl.BlockSpec(memory_space=pl.ANY)],
        out_specs=pl.BlockSpec(memory_space=pltpu.HBM),
        out_shape=jax.ShapeDtypeStruct((slots, part), emb.dtype),
        scratch_shapes=[
            pltpu.VMEM((local, part), emb.dtype),
            pltpu.VMEM((slots, part), emb.dtype),
            pltpu.SemaphoreType.DMA,
            pltpu.SemaphoreType.DMA((groups,)),
        ],
        cost_estimate=pl.CostEstimate(
            flops=2 * slots * local * part,
            bytes_accessed=2 * part * (slots + local),
            transcendentals=0,
        ),
        compiler_params=pltpu.CompilerParams(vmem_limit_bytes=BIG),
        name="gather_rows",
    )(ids, emb)


def place_body(blocks, half, info_ref, places_ref, rows_ref, *out_refs):
    arrivals = rows_ref.shape[0]
    here = info_ref[KC * 4 + HERE]
    places = places_ref[...]
    cluster = places // (2 * half)
    inner = places % (2 * half)
    toward = jnp.full_like(places, 8)
    for c in range(KC):
        toward = jnp.where(cluster == c, info_ref[KC * 4 + HOME + c] ^ here, toward)
    target = jnp.where(inner < half, toward * half + inner, 4 * half + inner - half)
    target = jnp.where(cluster < KC, target, -1)
    for ref, inside in zip(out_refs, blocks):
        for n, b in enumerate(inside):
            slot = b * half + lax.broadcasted_iota(jnp.int32, (half, arrivals), 0)
            pick = jnp.where(slot == target, 1.0, 0.0).astype(jnp.bfloat16)
            rows = jnp.dot(pick, rows_ref[...], preferred_element_type=jnp.float32)
            ref[n * half : (n + 1) * half, :] = rows.astype(jnp.bfloat16)


def place_rows(info, places, rows, half, blocks):
    arrivals, part = rows.shape
    sizes = [half * len(inside) for inside in blocks]
    return pl.pallas_call(
        functools.partial(place_body, blocks, half),
        in_specs=[smem, vmem, vmem],
        out_specs=(vmem,) * len(sizes),
        out_shape=tuple(jax.ShapeDtypeStruct((n, part), rows.dtype) for n in sizes),
        cost_estimate=pl.CostEstimate(
            flops=2 * arrivals * sum(sizes) * part,
            bytes_accessed=2 * part * (arrivals + sum(sizes)),
            transcendentals=0,
        ),
        compiler_params=pltpu.CompilerParams(vmem_limit_bytes=SMALL),
        name="place_rows",
    )(info, places, rows)


def read_plan(info_ref, half):
    base = KC * 4
    here = info_ref[base + HERE]
    mine = info_ref[base + MINE]
    blocks = []
    for x in range(4):
        rows = jnp.minimum(info_ref[(here ^ x) * KC + mine], half)
        blocks.append((rows, here ^ x, 0))
    over = [
        (OWN, here),
        (PAIR, here ^ 1),
        (STEP, info_ref[base + STEP_FROM]),
        (EXTRA, 3 - here),
    ]
    for valid, sender in over:
        blocks.append((info_ref[base + valid] * half, sender, half // LANES))
    return blocks


def spots(blocks, half, first):
    found, at = [], first
    for rows, _, _ in blocks:
        for h in range(half // LANES):
            filled = rows > h * LANES
            found.append((filled, at))
            at = at + filled.astype(jnp.int32)
    return found, at


def take_units(found, sources, parts, unit_b, total_sum):
    firsts = [sum(parts[:k]) for k in range(len(parts))]
    for (filled, at), refs in zip(found, sources):

        @pl.when(filled)
        def _(at=at, refs=refs):
            pieces = [ref[...].astype(jnp.float32) for ref in refs]
            square = sum(jnp.sum(x * x, axis=-1, keepdims=True) for x in pieces)
            inverse = lax.rsqrt(square + 1e-06)
            for x, first, part in zip(pieces, firsts, parts):
                cols = slice(first, first + part)
                total_sum[:, cols] += jnp.sum(x.reshape(LANES // 8, 8, part), axis=0)
                unit_b[pl.ds(pl.multiple_of(at * LANES, LANES), LANES), cols] = (
                    x * inverse
                ).astype(jnp.bfloat16)


def add_pairs(pairs_ref, first, end, last, hole, unit_b, similar_ref, row_acc, col_acc):
    key = lax.broadcasted_iota(jnp.int32, (ROWS, ROWS), 1)
    query = lax.broadcasted_iota(jnp.int32, (ROWS, ROWS), 0)
    ahead = key - query
    block_of = lambda i: pl.ds(pl.multiple_of(i * ROWS, ROWS), ROWS)

    def pair_of(s, h):
        t = first + s * UNROLL + h
        return pairs_ref[0, t], pairs_ref[1, t], t

    def multiply(s):
        for h in range(UNROLL):
            i, j, _ = pair_of(s, h)
            similar_ref[s % 2, h] = lax.dot_general(
                unit_b[block_of(i), :],
                unit_b[block_of(j), :],
                ACROSS,
                preferred_element_type=jnp.float32,
            )

    def accumulate(s):
        for h in range(UNROLL):
            i, j, t = pair_of(s, h)
            counted = key < jnp.where(t < end, last - j * ROWS, 0)
            counted &= ahead != (i - j) * ROWS
            if hole is not None:
                counted &= (query < hole[0] - i * ROWS) | (query >= hole[1] - i * ROWS)
            terms = jnp.where(counted, jnp.exp(SHARPNESS * similar_ref[s % 2, h]), 0.0)
            row_acc[block_of(i), :] += sum(
                terms[:, k * LANES : (k + 1) * LANES] for k in range(ROWS // LANES)
            )
            sums = jnp.sum(terms.reshape(ROWS // 8, 8, ROWS), axis=0)
            col_acc[:, block_of(j)] += jnp.where(i == j, 0.0, sums)

    steps = (end - first + UNROLL - 1) // UNROLL
    multiply(0)

    def step(s, carry):
        multiply(s)
        accumulate(s - 1)
        return carry

    lax.fori_loop(1, steps, step, 0)
    accumulate(steps - 1)


def start_body(parts, half, info_ref, pairs_ref, *refs):
    per_chunk = 5
    chunks = [refs[k * per_chunk : (k + 1) * per_chunk] for k in range(len(parts))]
    unit_b, row_acc, col_acc, total_sum, similar_ref = refs[len(parts) * per_chunk :]
    blocks = read_plan(info_ref, half)[:6]
    found, units = spots(blocks, half, jnp.int32(0))
    sources = []
    for which, at in [(0, 0), (2, 0), (3, 0), (4, 0), (1, half), (2, half)]:
        for h in range(half // LANES):
            rows = pl.ds(at + h * LANES, LANES)
            sources.append([chunk[which].at[rows] for chunk in chunks])
    total_sum[...] = jnp.zeros_like(total_sum)
    row_acc[...] = jnp.zeros_like(row_acc)
    col_acc[...] = jnp.zeros_like(col_acc)
    take_units(found, sources, parts, unit_b, total_sum)

    @pl.when(units % 2 == 1)
    def _():
        unit_b[pl.ds(pl.multiple_of(units * LANES, LANES), LANES), :] = jnp.zeros(
            (LANES, sum(parts)), jnp.bfloat16
        )

    count = (units + 1) // 2
    end = count * (count + 1) // 2
    add_pairs(
        pairs_ref, 0, end, units * LANES, None, unit_b, similar_ref, row_acc, col_acc
    )


def score_body(parts, half, info_ref, pairs_ref, *refs):
    per_chunk = 2
    chunks = [refs[k * per_chunk : (k + 1) * per_chunk] for k in range(len(parts))]
    refs = refs[len(parts) * per_chunk + 4 :]
    out_ref, unit_b, row_acc, col_acc, total_sum, similar_ref, score_ref = refs
    width = sum(parts)
    per_half = half // LANES
    blocks = read_plan(info_ref, half)
    found, early = spots(blocks[:6], half, jnp.int32(0))
    early_blocks = (early + 1) // 2
    late_found, units = spots(blocks[6:], half, early_blocks * 2)
    count_blocks = units // 2
    first = early_blocks * (early_blocks + 1) // 2
    end = count_blocks * (count_blocks + 1) // 2

    @pl.when(count_blocks > early_blocks)
    def _():
        sources = []
        for which in range(2):
            for h in range(per_half):
                rows = pl.ds(h * LANES, LANES)
                sources.append([chunk[which].at[rows] for chunk in chunks])
        take_units(late_found, sources, parts, unit_b, total_sum)
        hole = (early * LANES, early_blocks * ROWS)
        add_pairs(
            pairs_ref, first, end, units * LANES, hole, unit_b, similar_ref, row_acc, col_acc
        )

    filled_units = early + units - early_blocks * 2
    count = (filled_units * LANES).astype(jnp.float32)
    centroid = jnp.sum(total_sum[...], axis=0, keepdims=True) / count
    direction = centroid * lax.rsqrt(
        jnp.sum(centroid * centroid, axis=-1, keepdims=True) + 1e-06
    )
    high = direction.astype(jnp.bfloat16)
    low = (direction - high.astype(jnp.float32)).astype(jnp.bfloat16)
    row = lax.broadcasted_iota(jnp.int32, (8, width), 0)
    split = jnp.where(
        row == 0,
        high.astype(jnp.float32),
        jnp.where(row == 1, low.astype(jnp.float32), 0.0),
    ).astype(jnp.bfloat16)
    ones = jnp.ones((8, LANES), jnp.float32)
    for b in range(unit_b.shape[0] // ROWS):
        at = slice(b * ROWS, (b + 1) * ROWS)

        @pl.when(b < count_blocks)
        def _(at=at):
            along = lax.dot_general(
                split, unit_b[at, :], ACROSS, preferred_element_type=jnp.float32
            )
            toward = jnp.sum(along, axis=0, keepdims=True)
            rows = lax.dot_general(
                ones,
                row_acc[at, :],
                ACROSS,
                precision=lax.Precision.HIGHEST,
                preferred_element_type=jnp.float32,
            )
            total = rows[:1] + jnp.sum(col_acc[:, at], axis=0, keepdims=True)
            score_ref[:, at] = jnp.log(total) / SHARPNESS - toward

    for s in range(4):
        out_ref[s, : 2 * per_half, :] = jnp.zeros((2 * per_half, LANES), jnp.float32)
        for k in range(width // LANES):
            at = 2 * per_half + k
            out_ref[s, at : at + 1, :] = centroid[:, k * LANES : (k + 1) * LANES]
    for u, (filled, at) in enumerate(found + late_found):
        _, sender, place = blocks[u // per_half]

        @pl.when(filled)
        def _(at=at, to=sender, place=place + u % per_half):
            out_ref[to, place : place + 1, :] = score_ref[
                :, pl.ds(pl.multiple_of(at * LANES, LANES), LANES)
            ]


def start_cluster(info, chunks):
    half = chunks[0][0].shape[0]
    parts = [chunk[0].shape[1] for chunk in chunks]
    width = sum(parts)
    capacity = 8 * half
    flat = [a for chunk in chunks for a in chunk]
    return pl.pallas_call(
        functools.partial(start_body, parts, half),
        in_specs=[smem, smem] + [vmem] * len(flat),
        out_specs=(vmem,) * 4,
        out_shape=(
            jax.ShapeDtypeStruct((capacity, width), jnp.bfloat16),
            jax.ShapeDtypeStruct((capacity, LANES), jnp.float32),
            jax.ShapeDtypeStruct((8, capacity), jnp.float32),
            jax.ShapeDtypeStruct((8, width), jnp.float32),
        ),
        scratch_shapes=[pltpu.VMEM((2, UNROLL, ROWS, ROWS), jnp.float32)],
        cost_estimate=pl.CostEstimate(
            flops=capacity * capacity * width,
            bytes_accessed=2 * capacity * width,
            transcendentals=capacity * capacity // 2,
        ),
        compiler_params=pltpu.CompilerParams(vmem_limit_bytes=SMALL),
        name="start_cluster",
    )(info, jnp.asarray(pair_table(capacity // ROWS)), *flat)


def score_cluster(info, chunks, begun):
    half = chunks[0][0].shape[0]
    parts = [chunk[0].shape[1] for chunk in chunks]
    width = sum(parts)
    capacity = 8 * half
    flat = [a for chunk in chunks for a in chunk]
    lines = 2 * half // LANES + width // LANES
    at = 2 + len(flat)
    out = pl.pallas_call(
        functools.partial(score_body, parts, half),
        in_specs=[smem, smem] + [vmem] * (len(flat) + 4),
        out_specs=(vmem,) * 5,
        out_shape=(jax.ShapeDtypeStruct((4, lines, LANES), jnp.float32),)
        + tuple(jax.ShapeDtypeStruct(a.shape, a.dtype) for a in begun),
        input_output_aliases={at + n: 1 + n for n in range(4)},
        scratch_shapes=[
            pltpu.VMEM((2, UNROLL, ROWS, ROWS), jnp.float32),
            pltpu.VMEM((1, capacity), jnp.float32),
        ],
        cost_estimate=pl.CostEstimate(
            flops=capacity * capacity * width // 4,
            bytes_accessed=2 * capacity * width,
            transcendentals=capacity * capacity // 8,
        ),
        compiler_params=pltpu.CompilerParams(vmem_limit_bytes=SMALL),
        name="score_cluster",
    )(info, jnp.asarray(pair_table(capacity // ROWS)), *flat, *begun)
    return out[0]


def finish_body(info_ref, back_ref, centroid_ref, score_ref):
    per = score_ref.shape[1] // LANES
    for c in range(KC):
        home = info_ref[KC * 4 + HOME + c]
        for k in range(back_ref.shape[1]):
            to, at = (score_ref, k) if k < per else (centroid_ref, k - per)
            to[c : c + 1, at * LANES : (at + 1) * LANES] = back_ref[home, k : k + 1, :]


def finish(info, back, sub, width):
    return pl.pallas_call(
        finish_body,
        in_specs=[smem, vmem],
        out_specs=(vmem, vmem),
        out_shape=(
            jax.ShapeDtypeStruct((KC, width), jnp.float32),
            jax.ShapeDtypeStruct((KC, sub), jnp.float32),
        ),
        name="finish",
    )(info, back)


def swap(x, by):
    return lax.ppermute(x, "own", [(z, z ^ by) for z in range(4)])


def step_move(carried):
    return lax.ppermute(carried, "own", [(1, 2), (2, 1)])


def extra_move(overflow):
    owners = lax.axis_size("rows")
    crossing = [(r * 4 + 2 - r % 2, r * 4 + 1 + r % 2) for r in range(owners)]
    return lax.ppermute(overflow, ("rows", "own"), crossing)


def on_device(emb, send_rows, dest_offset):
    owners = lax.axis_size("rows")
    local, width = emb.shape
    slots = send_rows.shape[2]
    sub = local // 2
    half = sub // 2
    parts = [width // 8 * n for n in EIGHTHS]
    ids = send_rows[0].reshape(-1, ROWS)
    here = lax.axis_index("own")
    owner = lax.axis_index("rows")
    every = lax.all_to_all(
        jnp.repeat(dest_offset[0], 4, axis=0), ("rows", "own"), split_axis=0, concat_axis=0, tiled=True
    )
    every = every.reshape(owners, 4, slots)
    places = lax.dynamic_index_in_dim(every, here, 1, keepdims=False)
    places = places.reshape(1, owners * slots)
    cluster = jnp.arange(KC, dtype=jnp.int32)
    counts = jnp.sum((every[..., None] // sub == cluster).astype(jnp.int32), axis=(0, 2))
    place_value = jnp.asarray([64, 16, 4, 1], jnp.int32)
    index = jnp.sum(jnp.argmax(counts, axis=1).astype(jnp.int32) * place_value)
    index = ((owner % 2) * 256 + index) * 4 + here
    row = lax.dynamic_index_in_dim(jnp.asarray(PLANS), index, 0, keepdims=False)
    info = jnp.concatenate([counts.reshape(-1), row])

    tie = lax.optimization_barrier
    outgoing, moved, carried, steps = [], [], [], []

    def gather(k, ids):
        rows = gather_rows(ids, emb, sum(parts[:k]), parts[k])
        outgoing.append(rows.reshape(owners, slots, parts[k]))

    gather(0, ids)
    ids, info = tie((ids, info))
    gather(1, ids)
    extras = []
    for k, part in enumerate(parts):
        incoming = lax.all_to_all(outgoing[k], "rows", split_axis=0, concat_axis=0, tiled=True)
        incoming = incoming.reshape(owners * slots, part)
        if k:
            incoming, carried[-1] = tie((incoming, carried[-1]))
        two, three = place_rows(info, places, incoming, half, ((2,), (3,)))
        incoming, two = tie((incoming, two))
        kept, pair = place_rows(info, places, incoming, half, ((0,), (1, 4)))
        if k:
            steps.append(step_move(carried[-1]))
            two, three, pair, steps[-1], extras[-1], *last = tie(
                (two, three, pair, steps[-1], extras[-1]) + moved[-1]
            )
            moved[-1] = tuple(last)
        from_two, from_three, from_pair = swap(two, 2), swap(three, 3), swap(pair, 1)
        moved.append((kept, pair, from_pair, from_two, from_three))
        carried.append(
            jnp.where(info[KC * 4 + FORWARD] == 1, from_pair[half:], pair[half:])
        )
        overflow = pair[half:]
        if k == CHUNKS - 1:
            overflow, carried[-1] = tie((overflow, carried[-1]))
        extras.append(extra_move(overflow))
    steps.append(step_move(carried[-1]))
    begun = start_cluster(info, moved)
    result = score_cluster(info, list(zip(steps, extras)), begun)
    back = lax.all_to_all(result, "own", split_axis=0, concat_axis=0, tiled=True)
    return finish(info, back, sub, width)


def solution(mesh):
    return jax.shard_map(
        on_device,
        mesh=mesh,
        in_specs=(
            P(("rows", "own"), None),
            P(("rows", "own"), None, None),
            P(("rows", "own"), None, None),
        ),
        out_specs=(P("rows", None), P("rows", "own")),
        check_vma=False,
    )
```

profile of v0, /device:TPU:0, one launch (start us, length us, event | category | flops | bytes accessed | tf_op | source)
XLA Modules:
  0.0 139.8 jit_solution(3944802257974825178)
XLA Ops:
  0.6 0.7 broadcast_in_dim.4
  1.3 0.6 all_to_all.15
  2.0 7.3 %all-to-all-start = ((s32[32,1,256]{2,1,0:T(1,128)}), s32[32,1,256]{2,1,0:T(1,128)S(1)}, u32[]{:S(2)}, u32[]{:S(2)}) async-start(s32[32,1,256]{2,1,0:T(1,128)} %all_to_all.15), calls=%async_computation | async-start | bytes 65536 | tf_op jit(solution)/shard_map/all_to_all | solution.py:475
  9.3 5.1 %gather_rows.3 = bf16[2048,512]{1,0:T(8,128)(2,1)} custom-call(s32[8,256]{1,0:T(8,128)} %bitcast.19, bf16[1024,1024]{1,0:T(8,128)(2,1)} %emb_ref.3), custom_call_target="tpu_custom_call" | custom-call | flops 2147483648 | bytes 3145728 | tf_op jit(solution)/shard_map/gather_rows/pallas_call | solution.py:116
  14.4 2.2 %all-to-all-done = s32[32,1,256]{2,1,0:T(1,128)S(1)} async-done(((s32[32,1,256]{2,1,0:T(1,128)}), s32[32,1,256]{2,1,0:T(1,128)S(1)}, u32[]{:S(2)}, u32[]{:S(2)}) %all-to-all-start) | async-done | bytes 32800 | tf_op jit(solution)/shard_map/all_to_all | solution.py:475
  16.6 0.0 copy-start.2
  16.6 3.7 %all-to-all-start.2 = ((bf16[8,256,512]{2,1,0:T(8,128)(2,1)}), bf16[8,256,512]{2,1,0:T(8,128)(2,1)S(1)}, u32[]{:S(2)}, u32[]{:S(2)}) async-start(bf16[8,256,512]{2,1,0:T(8,128)(2,1)} %bitcast.16), calls=%async_computation.2 | async-start | bytes 4194304 | tf_op jit(solution)/shard_map/all_to_all | solution.py:501
  20.3 0.1 reduce.18
  20.5 0.4 convert_reduce_fusion
  20.9 0.1 reshape.97
  21.0 0.6 iota_reduce_fusion
  21.6 0.0 copy-done.2
  21.6 0.6 multiply_reduce_fusion
  22.9 0.7 dynamic-slice_bitcast_fusion
  23.6 0.1 pad_add_fusion.info_ref
  23.7 0.0 copy-start
  23.7 5.1 %gather_rows.2 = bf16[2048,512]{1,0:T(8,128)(2,1)} custom-call(s32[8,256]{1,0:T(8,128)} %bitcast.20, bf16[1024,1024]{1,0:T(8,128)(2,1)} %emb_ref.3), custom_call_target="tpu_custom_call" | custom-call | flops 2147483648 | bytes 3145728 | tf_op jit(solution)/shard_map/gather_rows/pallas_call | solution.py:116
  28.8 18.1 %all-to-all-done.2 = bf16[8,256,512]{2,1,0:T(8,128)(2,1)S(1)} async-done(((bf16[8,256,512]{2,1,0:T(8,128)(2,1)}), bf16[8,256,512]{2,1,0:T(8,128)(2,1)S(1)}, u32[]{:S(2)}, u32[]{:S(2)}) %all-to-all-start.2) | async-done | bytes 2097184 | tf_op jit(solution)/shard_map/all_to_all | solution.py:501
  46.9 4.3 %all-to-all-start.1 = ((bf16[8,256,512]{2,1,0:T(8,128)(2,1)}), bf16[8,256,512]{2,1,0:T(8,128)(2,1)}, u32[]{:S(2)}, u32[]{:S(2)}) async-start(bf16[8,256,512]{2,1,0:T(8,128)(2,1)} %bitcast.17), calls=%async_computation.1 | async-start | bytes 4194304 | tf_op jit(solution)/shard_map/all_to_all | solution.py:501
  51.3 1.8 %place_rows.4 = (bf16[256,512]{1,0:T(8,128)(2,1)S(1)}, bf16[256,512]{1,0:T(8,128)(2,1)S(1)}) custom-call(s32[32]{0:T(128)S(1)} %pad_add_fusion.info_ref, s32[1,2048]{1,0:T(1,128)S(1)} %bitcast.12, bf16[2048,512]{1,0:T(8,128)(2,1)S(1)} %bitcast.10), custom_call_target="tpu_custom_call" | custom-call | flops 1073741824 | bytes 2621440 | tf_op jit(solution)/shard_map/place_rows/pallas_call | solution.py:159
  53.1 2.3 %place_rows.5 = (bf16[256,512]{1,0:T(8,128)(2,1)S(1)}, bf16[512,512]{1,0:T(8,128)(2,1)S(1)}) custom-call(s32[32]{0:T(128)S(1)} %pad_add_fusion.info_ref, s32[1,2048]{1,0:T(1,128)S(1)} %bitcast.13, bf16[2048,512]{1,0:T(8,128)(2,1)S(1)} %bitcast.11), custom_call_target="tpu_custom_call" | custom-call | flops 1610612736 | bytes 2883584 | tf_op jit(solution)/shard_map/place_rows/pallas_call | solution.py:159
  55.4 0.5 collective-permute-start
  55.9 0.6 slice.18
  57.1 1.7 %collective-permute-start.3 = (bf16[256,512]{1,0:T(8,128)(2,1)S(1)}, bf16[256,512]{1,0:T(8,128)(2,1)S(1)}, u32[]{:S(2)}, u32[]{:S(2)}) collective-permute-start(bf16[256,512]{1,0:T(8,128)(2,1)S(1)} %get-tuple-element.50), channel_id=1, source_target_pairs={{0,2},{1,3},{2,0},{3,1},{4,6},{5,7},{6,4},{7,5},{8,10},{9,11},{10,... | collective-permute-start | bytes 786440 | tf_op jit(solution)/shard_map/ppermute | solution.py:452
  58.8 2.4 %collective-permute-start.4 = (bf16[256,512]{1,0:T(8,128)(2,1)S(1)}, bf16[256,512]{1,0:T(8,128)(2,1)S(1)}, u32[]{:S(2)}, u32[]{:S(2)}) collective-permute-start(bf16[256,512]{1,0:T(8,128)(2,1)S(1)} %get-tuple-element.51), channel_id=1, source_target_pairs={{0,3},{1,2},{2,1},{3,0},{4,7},{5,6},{6,5},{7,4},{8,11},{9,10},{10,... | collective-permute-start | bytes 786440 | tf_op jit(solution)/shard_map/ppermute | solution.py:452
  61.2 14.6 %collective-permute-done.refs_2_ = bf16[512,512]{1,0:T(8,128)(2,1)S(1)} collective-permute-done((bf16[512,512]{1,0:T(8,128)(2,1)S(1)}, bf16[512,512]{1,0:T(8,128)(2,1)S(1)}, u32[]{:S(2)}, u32[]{:S(2)}) %collective-permute-start) | collective-permute-done | bytes 524320 | tf_op jit(solution)/shard_map/ppermute | solution.py:452
  75.8 0.8 fusion.2
  76.6 1.3 all-to-all-done.1
  77.9 0.7 collective-permute-start.1
  78.6 0.7 collective-permute-start.2
  79.3 2.8 %place_rows.6 = (bf16[256,512]{1,0:T(8,128)(2,1)S(1)}, bf16[256,512]{1,0:T(8,128)(2,1)S(1)}) custom-call(s32[32]{0:T(128)S(1)} %pad_add_fusion.info_ref, s32[1,2048]{1,0:T(1,128)S(1)} %bitcast.14, bf16[2048,512]{1,0:T(8,128)(2,1)} %bitcast.4.rows_ref), custom_call_target="tpu_custom_call" | custom-call | flops 1073741824 | bytes 2621440 | tf_op jit(solution)/shard_map/place_rows/pallas_call | solution.py:159
  82.1 0.0 copy-start.1
  82.1 3.4 %place_rows.7 = (bf16[256,512]{1,0:T(8,128)(2,1)S(1)}, bf16[512,512]{1,0:T(8,128)(2,1)S(1)}) custom-call(s32[32]{0:T(128)S(1)} %pad_add_fusion.info_ref, s32[1,2048]{1,0:T(1,128)S(1)} %bitcast.15, bf16[2048,512]{1,0:T(8,128)(2,1)} %bitcast.4.rows_ref), custom_call_target="tpu_custom_call" | custom-call | flops 1610612736 | bytes 2883584 | tf_op jit(solution)/shard_map/place_rows/pallas_call | solution.py:159
  85.5 0.0 collective-permute-done.3.refs_3_
  85.5 0.0 collective-permute-done.4.refs_4_
  85.5 0.0 collective-permute-done.1.refs_0_
  85.5 0.0 collective-permute-done.2.refs_1_
  85.6 6.7 %collective-permute-start.5 = (bf16[512,512]{1,0:T(8,128)(2,1)S(1)}, bf16[512,512]{1,0:T(8,128)(2,1)S(1)}, u32[]{:S(2)}, u32[]{:S(2)}) collective-permute-start(bf16[512,512]{1,0:T(8,128)(2,1)S(1)} %get-tuple-element.54.refs_6_), channel_id=1, source_target_pairs={{0,1},{1,0},{2,3},{3,2},{4,5},{5,4},{6,7},{7,6},{8,9},{9,8},{10,11... | collective-permute-start | bytes 1572872 | tf_op jit(solution)/shard_map/ppermute | solution.py:452
  92.2 0.0 collective-permute-start.8
  92.2 2.4 %collective-permute-start.9 = (bf16[256,512]{1,0:T(8,128)(2,1)S(1)}, bf16[256,512]{1,0:T(8,128)(2,1)S(1)}, u32[]{:S(2)}, u32[]{:S(2)}) collective-permute-start(bf16[256,512]{1,0:T(8,128)(2,1)S(1)} %get-tuple-element.64), channel_id=1, source_target_pairs={{0,3},{1,2},{2,1},{3,0},{4,7},{5,6},{6,5},{7,4},{8,11},{9,10},{10,... | collective-permute-start | bytes 786440 | tf_op jit(solution)/shard_map/ppermute | solution.py:452
  94.6 13.8 %collective-permute-done.5.refs_7_ = bf16[512,512]{1,0:T(8,128)(2,1)S(1)} collective-permute-done((bf16[512,512]{1,0:T(8,128)(2,1)S(1)}, bf16[512,512]{1,0:T(8,128)(2,1)S(1)}, u32[]{:S(2)}, u32[]{:S(2)}) %collective-permute-start.5) | collective-permute-done | bytes 524320 | tf_op jit(solution)/shard_map/ppermute | solution.py:452
  108.4 0.7 collective-permute-start.6
  109.1 0.7 collective-permute-start.7
  109.8 0.5 collective-permute-done.8.refs_8_
  110.3 6.5 %collective-permute-done.9.refs_9_ = bf16[256,512]{1,0:T(8,128)(2,1)S(1)} collective-permute-done((bf16[256,512]{1,0:T(8,128)(2,1)S(1)}, bf16[256,512]{1,0:T(8,128)(2,1)S(1)}, u32[]{:S(2)}, u32[]{:S(2)}) %collective-permute-start.9) | collective-permute-done | bytes 262176 | tf_op jit(solution)/shard_map/ppermute | solution.py:452
  116.8 0.0 copy-done.1
  116.8 5.4 %start_cluster.1 = (bf16[2048,1024]{1,0:T(8,128)(2,1)S(1)}, f32[2048,128]{1,0:T(8,128)S(1)}, f32[8,2048]{1,0:T(8,128)S(1)}, f32[8,1024]{1,0:T(8,128)S(1)}) custom-call(s32[32]{0:T(128)S(1)} %pad_add_fusion.info_ref, s32[2,40]{1,0:T(2,128)S(1)} %copy-done.1, bf16[256,512]{1,0:T(8,128)(2,1)S(1)} %get-tuple-element.57.refs_0_, ...), custom_call_target="tpu_custom_call" | custom-call | flops 4294967296 | bytes 4194304 | tf_op jit(solution)/shard_map/start_cluster/pallas_call | solution.py:378
  122.2 0.0 collective-permute-done.6.refs_2_
  122.2 0.0 collective-permute-done.7.refs_3_
  122.2 0.0 copy-done
  122.2 2.3 %score_cluster.1 = (f32[4,12,128]{2,1,0:T(8,128)S(1)}, bf16[2048,1024]{1,0:T(8,128)(2,1)S(1)}, f32[2048,128]{1,0:T(8,128)S(1)}, f32[8,2048]{1,0:T(8,128)S(1)}, f32[8,1024]{1,0:T(8,128)S(1)}) custom-call(s32[32]{0:T(128)S(1)} %pad_add_fusion.info_ref, s32[2,40]{1,0:T(2,128)S(1)} %copy-done.1, ...), custom_call_target="tpu_custom_call", output_to_operand_aliasing={{1}: (6, {}), {2}: (7, {}), {3}: (8, {}), {4}: (9, {})} | custom-call | flops 1073741824 | bytes 4194304 | tf_op jit(solution)/shard_map/score_cluster/pallas_call | solution.py:407
  124.5 13.9 %all_to_all.24.back_ref = f32[4,12,128]{2,1,0:T(8,128)} all-to-all(f32[4,12,128]{2,1,0:T(8,128)S(1)} %get-tuple-element.69), channel_id=1, replica_groups=mesh['rows'=8,'own'=4] {'own'}, dimensions={0} | all-to-all | bytes 49152 | tf_op jit(solution)/shard_map/all_to_all | solution.py:526
  138.4 1.4 finish.1
  (5 shorter events, 0.1 us)
Async XLA Ops:
  2.0 14.6 %all-to-all-start = ((s32[32,1,256]{2,1,0:T(1,128)}), s32[32,1,256]{2,1,0:T(1,128)S(1)}, u32[]{:S(2)}, u32[]{:S(2)}) async-start(s32[32,1,256]{2,1,0:T(1,128)} %all_to_all.15), calls=%async_computation | async-start | bytes 65536 | tf_op jit(solution)/shard_map/all_to_all | solution.py:475
  16.6 5.0 %copy-start.2 = (s32[4]{0:T(128)S(1)}, s32[4]{0:T(128)}, u32[]{:S(2)}) copy-start(s32[4]{0:T(128)} %constant.64.clone) | copy-start | bytes 52
  16.6 30.3 %all-to-all-start.2 = ((bf16[8,256,512]{2,1,0:T(8,128)(2,1)}), bf16[8,256,512]{2,1,0:T(8,128)(2,1)S(1)}, u32[]{:S(2)}, u32[]{:S(2)}) async-start(bf16[8,256,512]{2,1,0:T(8,128)(2,1)} %bitcast.16), calls=%async_computation.2 | async-start | bytes 4194304 | tf_op jit(solution)/shard_map/all_to_all | solution.py:501
  23.7 98.5 %copy-start = (s32[32]{0:T(128)}, s32[32]{0:T(128)S(1)}, u32[]{:S(2)}) copy-start(s32[32]{0:T(128)S(1)} %pad_add_fusion.info_ref) | copy-start | bytes 388
  46.9 31.0 %all-to-all-start.1 = ((bf16[8,256,512]{2,1,0:T(8,128)(2,1)}), bf16[8,256,512]{2,1,0:T(8,128)(2,1)}, u32[]{:S(2)}, u32[]{:S(2)}) async-start(bf16[8,256,512]{2,1,0:T(8,128)(2,1)} %bitcast.17), calls=%async_computation.1 | async-start | bytes 4194304 | tf_op jit(solution)/shard_map/all_to_all | solution.py:501
  55.4 20.4 %collective-permute-start = (bf16[512,512]{1,0:T(8,128)(2,1)S(1)}, bf16[512,512]{1,0:T(8,128)(2,1)S(1)}, u32[]{:S(2)}, u32[]{:S(2)}) collective-permute-start(bf16[512,512]{1,0:T(8,128)(2,1)S(1)} %get-tuple-element.58.refs_1_), channel_id=1, source_target_pairs={{0,1},{1,0},{2,3},{3,2},{4,5},{5,4},{6,7},{7,6},{8,9},{9,8},{10,11... | collective-permute-start | bytes 1572872 | tf_op jit(solution)/shard_map/ppermute | solution.py:452
  57.1 28.4 %collective-permute-start.3 = (bf16[256,512]{1,0:T(8,128)(2,1)S(1)}, bf16[256,512]{1,0:T(8,128)(2,1)S(1)}, u32[]{:S(2)}, u32[]{:S(2)}) collective-permute-start(bf16[256,512]{1,0:T(8,128)(2,1)S(1)} %get-tuple-element.50), channel_id=1, source_target_pairs={{0,2},{1,3},{2,0},{3,1},{4,6},{5,7},{6,4},{7,5},{8,10},{9,11},{10,... | collective-permute-start | bytes 786440 | tf_op jit(solution)/shard_map/ppermute | solution.py:452
  58.8 26.7 %collective-permute-start.4 = (bf16[256,512]{1,0:T(8,128)(2,1)S(1)}, bf16[256,512]{1,0:T(8,128)(2,1)S(1)}, u32[]{:S(2)}, u32[]{:S(2)}) collective-permute-start(bf16[256,512]{1,0:T(8,128)(2,1)S(1)} %get-tuple-element.51), channel_id=1, source_target_pairs={{0,3},{1,2},{2,1},{3,0},{4,7},{5,6},{6,5},{7,4},{8,11},{9,10},{10,... | collective-permute-start | bytes 786440 | tf_op jit(solution)/shard_map/ppermute | solution.py:452
  77.9 7.6 %collective-permute-start.1 = (bf16[256,512]{1,0:T(8,128)(2,1)}, bf16[256,512]{1,0:T(8,128)(2,1)S(1)}, u32[]{:S(2)}, u32[]{:S(2)}) collective-permute-start(bf16[256,512]{1,0:T(8,128)(2,1)} %get-tuple-element.48), channel_id=1, source_target_pairs={{1,2},{2,1},{5,6},{6,5},{9,10},{10,9},{13,14},{14,13},{17,18},{18,... | collective-permute-start | bytes 786440 | tf_op jit(solution)/shard_map/ppermute | solution.py:456
  78.6 7.0 %collective-permute-start.2 = (bf16[256,512]{1,0:T(8,128)(2,1)}, bf16[256,512]{1,0:T(8,128)(2,1)S(1)}, u32[]{:S(2)}, u32[]{:S(2)}) collective-permute-start(bf16[256,512]{1,0:T(8,128)(2,1)} %get-tuple-element.72), channel_id=1, source_target_pairs={{2,1},{5,6},{10,9},{13,14},{18,17},{21,22},{26,25},{29,30}} | collective-permute-start | bytes 786440 | tf_op jit(solution)/shard_map/ppermute | solution.py:462
  82.1 34.7 %copy-start.1 = (s32[2,40]{1,0:T(2,128)S(1)}, s32[2,40]{1,0:T(2,128)}, u32[]{:S(2)}) copy-start(s32[2,40]{1,0:T(2,128)} %constant.66.clone.pairs_ref) | copy-start | bytes 964
  85.6 22.8 %collective-permute-start.5 = (bf16[512,512]{1,0:T(8,128)(2,1)S(1)}, bf16[512,512]{1,0:T(8,128)(2,1)S(1)}, u32[]{:S(2)}, u32[]{:S(2)}) collective-permute-start(bf16[512,512]{1,0:T(8,128)(2,1)S(1)} %get-tuple-element.54.refs_6_), channel_id=1, source_target_pairs={{0,1},{1,0},{2,3},{3,2},{4,5},{5,4},{6,7},{7,6},{8,9},{9,8},{10,11... | collective-permute-start | bytes 1572872 | tf_op jit(solution)/shard_map/ppermute | solution.py:452
  92.2 18.0 %collective-permute-start.8 = (bf16[256,512]{1,0:T(8,128)(2,1)S(1)}, bf16[256,512]{1,0:T(8,128)(2,1)S(1)}, u32[]{:S(2)}, u32[]{:S(2)}) collective-permute-start(bf16[256,512]{1,0:T(8,128)(2,1)S(1)} %get-tuple-element.63), channel_id=1, source_target_pairs={{0,2},{1,3},{2,0},{3,1},{4,6},{5,7},{6,4},{7,5},{8,10},{9,11},{10,... | collective-permute-start | bytes 786440 | tf_op jit(solution)/shard_map/ppermute | solution.py:452
  92.2 24.5 %collective-permute-start.9 = (bf16[256,512]{1,0:T(8,128)(2,1)S(1)}, bf16[256,512]{1,0:T(8,128)(2,1)S(1)}, u32[]{:S(2)}, u32[]{:S(2)}) collective-permute-start(bf16[256,512]{1,0:T(8,128)(2,1)S(1)} %get-tuple-element.64), channel_id=1, source_target_pairs={{0,3},{1,2},{2,1},{3,0},{4,7},{5,6},{6,5},{7,4},{8,11},{9,10},{10,... | collective-permute-start | bytes 786440 | tf_op jit(solution)/shard_map/ppermute | solution.py:452
  108.4 13.8 %collective-permute-start.6 = (bf16[256,512]{1,0:T(8,128)(2,1)S(1)}, bf16[256,512]{1,0:T(8,128)(2,1)S(1)}, u32[]{:S(2)}, u32[]{:S(2)}) collective-permute-start(bf16[256,512]{1,0:T(8,128)(2,1)S(1)} %get-tuple-element.55), channel_id=1, source_target_pairs={{1,2},{2,1},{5,6},{6,5},{9,10},{10,9},{13,14},{14,13},{17,18},{18,... | collective-permute-start | bytes 786440 | tf_op jit(solution)/shard_map/ppermute | solution.py:456
  109.1 13.1 %collective-permute-start.7 = (bf16[256,512]{1,0:T(8,128)(2,1)S(1)}, bf16[256,512]{1,0:T(8,128)(2,1)S(1)}, u32[]{:S(2)}, u32[]{:S(2)}) collective-permute-start(bf16[256,512]{1,0:T(8,128)(2,1)S(1)} %get-tuple-element.56), channel_id=1, source_target_pairs={{2,1},{5,6},{10,9},{13,14},{18,17},{21,22},{26,25},{29,30}} | collective-permute-start | bytes 786440 | tf_op jit(solution)/shard_map/ppermute | solution.py:462
where the time goes:
time: 141 us; the launch traced here: 140 us
  waiting for transfers between devices  57 us (40%)
  starting transfers between devices  31.6 us (22%)
  Pallas kernels  29.6 us (21%)
  blocking collectives  13.9 us (10%)
  local copies, waits for them, and re-layouts  2.76 us (2%)
  other arithmetic  2.71 us (2%)
  between operations  2.19 us (2%)
    ppermute x6, waiting for transfers between devices, swap(): return lax.ppermute(x, 'own', [(z, z ^ by) for z in range(4)])  35.4 us
    all_to_all x2, waiting for transfers between devices, on_device(): lax.all_to_all(outgoing[k], 'rows', split_axis=0, concat_axis=0, tiled=True)  19.4 us
    all_to_all x1, blocking collectives, on_device(): lax.all_to_all(result, 'own', split_axis=0, concat_axis=0, tiled=True)  13.9 us
    ppermute x6, starting transfers between devices, swap(): return lax.ppermute(x, 'own', [(z, z ^ by) for z in range(4)])  13.6 us
    pallas_call x4, Pallas kernels, place_rows(): pl.pallas_call(functools.partial(place_body, blocks, half), in_specs=[sme...  10.3 us
    pallas_call x2, Pallas kernels, gather_rows(): pl.pallas_call(functools.partial(gather_body, first), in_specs=[vmem, pl....  10.1 us
    all_to_all x2, starting transfers between devices, on_device(): lax.all_to_all(outgoing[k], 'rows', split_axis=0, concat_axis=0, tiled=True)  8.07 us
    all_to_all x1, starting transfers between devices, on_device(): lax.all_to_all(jnp.repeat(dest_offset[0], 4, axis=0), ('rows', 'own'), sp...  7.3 us
  transfers between devices with their start and end apart: 13, of which 7 were waited for; matrix products, arithmetic and copies ran while one was open for 3% of the time, Pallas kernels for 18%

commit v1 on v0

--- a/solution.py
+++ b/solution.py
@@ -507,8 +507,8 @@
         kept, pair = place_rows(info, places, incoming, half, ((0,), (1, 4)))
         if k:
             steps.append(step_move(carried[-1]))
-            two, three, pair, steps[-1], extras[-1], *last = tie(
-                (two, three, pair, steps[-1], extras[-1]) + moved[-1]
+            two, three, pair, steps[-1], *last = tie(
+                (two, three, pair, steps[-1]) + moved[-1]
             )
             moved[-1] = tuple(last)
         from_two, from_three, from_pair = swap(two, 2), swap(three, 3), swap(pair, 1)
@@ -516,11 +516,9 @@
         carried.append(
             jnp.where(info[KC * 4 + FORWARD] == 1, from_pair[half:], pair[half:])
         )
-        overflow = pair[half:]
-        if k == CHUNKS - 1:
-            overflow, carried[-1] = tie((overflow, carried[-1]))
-        extras.append(extra_move(overflow))
     steps.append(step_move(carried[-1]))
+    first = moved[-1][2]
+    extras = [extra_move(tie((m[1][half:], first))[0]) for m in moved]
     begun = start_cluster(info, moved)
     result = score_cluster(info, list(zip(steps, extras)), begun)
     back = lax.all_to_all(result, "own", split_axis=0, concat_axis=0, tiled=True)

time: 141 us -> 141 us (level)
  blocking collectives: 13.9 us -> 17.5 us
  starting transfers between devices: 31.6 us -> 29.5 us
    all_to_all x1, blocking collectives: 13.9 us -> 17.5 us  [on_device(): lax.all_to_all(result, 'own', split_axis=0, concat_axis=0, tiled=True)]
    ppermute x6, starting transfers between devices: 13.6 us -> 11.5 us  [swap(): return lax.ppermute(x, 'own', [(z, z ^ by) for z in range(4)])]
  transfers between devices with their start and end apart: 13 -> 13, of which waited for: 7 -> 6; matrix products, arithmetic and copies ran while one was open for 3% -> 3% of each run, Pallas kernels for 18% -> 18%
where the time goes in v1:
time: 141 us; the launch traced here: 140 us
  waiting for transfers between devices  55.8 us (40%)
  Pallas kernels  29.6 us (21%)
  starting transfers between devices  29.5 us (21%)
  blocking collectives  17.5 us (12%)
  local copies, waits for them, and re-layouts  2.79 us (2%)
  other arithmetic  2.62 us (2%)
  between operations  2.21 us (2%)
    ppermute x6, waiting for transfers between devices, swap(): return lax.ppermute(x, 'own', [(z, z ^ by) for z in range(4)])  34.1 us
    all_to_all x2, waiting for transfers between devices, on_device(): lax.all_to_all(outgoing[k], 'rows', split_axis=0, concat_axis=0, tiled=True)  19.5 us
    all_to_all x1, blocking collectives, on_device(): lax.all_to_all(result, 'own', split_axis=0, concat_axis=0, tiled=True)  17.5 us
    ppermute x6, starting transfers between devices, swap(): return lax.ppermute(x, 'own', [(z, z ^ by) for z in range(4)])  11.5 us
    pallas_call x4, Pallas kernels, place_rows(): pl.pallas_call(functools.partial(place_body, blocks, half), in_specs=[sme...  10.3 us
    pallas_call x2, Pallas kernels, gather_rows(): pl.pallas_call(functools.partial(gather_body, first), in_specs=[vmem, pl....  10.1 us
    all_to_all x2, starting transfers between devices, on_device(): lax.all_to_all(outgoing[k], 'rows', split_axis=0, concat_axis=0, tiled=True)  8.08 us
    all_to_all x1, starting transfers between devices, on_device(): lax.all_to_all(jnp.repeat(dest_offset[0], 4, axis=0), ('rows', 'own'), sp...  7.3 us
  transfers between devices with their start and end apart: 13, of which 6 were waited for; matrix products, arithmetic and copies ran while one was open for 3% of the time, Pallas kernels for 18%

profile of v1, /device:TPU:0, one launch (start us, length us, event | category | flops | bytes accessed | tf_op | source)
XLA Modules:
  0.0 140.0 jit_solution(13400197748190752285)
XLA Ops:
  0.6 0.7 broadcast_in_dim.4
  1.3 0.7 all_to_all.15
  2.0 7.3 %all-to-all-start = ((s32[32,1,256]{2,1,0:T(1,128)}), s32[32,1,256]{2,1,0:T(1,128)S(1)}, u32[]{:S(2)}, u32[]{:S(2)}) async-start(s32[32,1,256]{2,1,0:T(1,128)} %all_to_all.15), calls=%async_computation | async-start | bytes 65536 | tf_op jit(solution)/shard_map/all_to_all | solution.py:475
  9.3 5.1 %gather_rows.3 = bf16[2048,512]{1,0:T(8,128)(2,1)} custom-call(s32[8,256]{1,0:T(8,128)} %bitcast.19, bf16[1024,1024]{1,0:T(8,128)(2,1)} %emb_ref.3), custom_call_target="tpu_custom_call" | custom-call | flops 2147483648 | bytes 3145728 | tf_op jit(solution)/shard_map/gather_rows/pallas_call | solution.py:116
  14.4 2.2 %all-to-all-done = s32[32,1,256]{2,1,0:T(1,128)S(1)} async-done(((s32[32,1,256]{2,1,0:T(1,128)}), s32[32,1,256]{2,1,0:T(1,128)S(1)}, u32[]{:S(2)}, u32[]{:S(2)}) %all-to-all-start) | async-done | bytes 32800 | tf_op jit(solution)/shard_map/all_to_all | solution.py:475
  16.6 0.0 copy-start.2
  16.6 3.7 %all-to-all-start.2 = ((bf16[8,256,512]{2,1,0:T(8,128)(2,1)}), bf16[8,256,512]{2,1,0:T(8,128)(2,1)S(1)}, u32[]{:S(2)}, u32[]{:S(2)}) async-start(bf16[8,256,512]{2,1,0:T(8,128)(2,1)} %bitcast.16), calls=%async_computation.2 | async-start | bytes 4194304 | tf_op jit(solution)/shard_map/all_to_all | solution.py:501
  20.3 0.1 reduce.18
  20.5 0.4 convert_reduce_fusion
  20.9 0.1 reshape.97
  21.0 0.6 iota_reduce_fusion
  21.6 0.0 copy-done.2
  21.6 0.6 multiply_reduce_fusion
  22.9 0.7 dynamic-slice_bitcast_fusion
  23.6 0.1 pad_add_fusion.info_ref
  23.7 0.0 copy-start
  23.7 5.1 %gather_rows.2 = bf16[2048,512]{1,0:T(8,128)(2,1)} custom-call(s32[8,256]{1,0:T(8,128)} %bitcast.20, bf16[1024,1024]{1,0:T(8,128)(2,1)} %emb_ref.3), custom_call_target="tpu_custom_call" | custom-call | flops 2147483648 | bytes 3145728 | tf_op jit(solution)/shard_map/gather_rows/pallas_call | solution.py:116
  28.8 18.1 %all-to-all-done.2 = bf16[8,256,512]{2,1,0:T(8,128)(2,1)S(1)} async-done(((bf16[8,256,512]{2,1,0:T(8,128)(2,1)}), bf16[8,256,512]{2,1,0:T(8,128)(2,1)S(1)}, u32[]{:S(2)}, u32[]{:S(2)}) %all-to-all-start.2) | async-done | bytes 2097184 | tf_op jit(solution)/shard_map/all_to_all | solution.py:501
  46.9 4.3 %all-to-all-start.1 = ((bf16[8,256,512]{2,1,0:T(8,128)(2,1)}), bf16[8,256,512]{2,1,0:T(8,128)(2,1)}, u32[]{:S(2)}, u32[]{:S(2)}) async-start(bf16[8,256,512]{2,1,0:T(8,128)(2,1)} %bitcast.17), calls=%async_computation.1 | async-start | bytes 4194304 | tf_op jit(solution)/shard_map/all_to_all | solution.py:501
  51.3 1.8 %place_rows.4 = (bf16[256,512]{1,0:T(8,128)(2,1)S(1)}, bf16[256,512]{1,0:T(8,128)(2,1)S(1)}) custom-call(s32[32]{0:T(128)S(1)} %pad_add_fusion.info_ref, s32[1,2048]{1,0:T(1,128)S(1)} %bitcast.12, bf16[2048,512]{1,0:T(8,128)(2,1)S(1)} %bitcast.10), custom_call_target="tpu_custom_call" | custom-call | flops 1073741824 | bytes 2621440 | tf_op jit(solution)/shard_map/place_rows/pallas_call | solution.py:159
  53.1 2.3 %place_rows.5 = (bf16[256,512]{1,0:T(8,128)(2,1)S(1)}, bf16[512,512]{1,0:T(8,128)(2,1)S(1)}) custom-call(s32[32]{0:T(128)S(1)} %pad_add_fusion.info_ref, s32[1,2048]{1,0:T(1,128)S(1)} %bitcast.13, bf16[2048,512]{1,0:T(8,128)(2,1)S(1)} %bitcast.11), custom_call_target="tpu_custom_call" | custom-call | flops 1610612736 | bytes 2883584 | tf_op jit(solution)/shard_map/place_rows/pallas_call | solution.py:159
  55.4 0.5 collective-permute-start
  55.9 0.6 slice.20
  57.1 1.7 %collective-permute-start.2 = (bf16[256,512]{1,0:T(8,128)(2,1)S(1)}, bf16[256,512]{1,0:T(8,128)(2,1)S(1)}, u32[]{:S(2)}, u32[]{:S(2)}) collective-permute-start(bf16[256,512]{1,0:T(8,128)(2,1)S(1)} %get-tuple-element.49), channel_id=1, source_target_pairs={{0,2},{1,3},{2,0},{3,1},{4,6},{5,7},{6,4},{7,5},{8,10},{9,11},{10,... | collective-permute-start | bytes 786440 | tf_op jit(solution)/shard_map/ppermute | solution.py:452
  58.8 2.4 %collective-permute-start.3 = (bf16[256,512]{1,0:T(8,128)(2,1)S(1)}, bf16[256,512]{1,0:T(8,128)(2,1)S(1)}, u32[]{:S(2)}, u32[]{:S(2)}) collective-permute-start(bf16[256,512]{1,0:T(8,128)(2,1)S(1)} %get-tuple-element.50), channel_id=1, source_target_pairs={{0,3},{1,2},{2,1},{3,0},{4,7},{5,6},{6,5},{7,4},{8,11},{9,10},{10,... | collective-permute-start | bytes 786440 | tf_op jit(solution)/shard_map/ppermute | solution.py:452
  61.2 14.6 %collective-permute-done.refs_2_ = bf16[512,512]{1,0:T(8,128)(2,1)S(1)} collective-permute-done((bf16[512,512]{1,0:T(8,128)(2,1)S(1)}, bf16[512,512]{1,0:T(8,128)(2,1)S(1)}, u32[]{:S(2)}, u32[]{:S(2)}) %collective-permute-start) | collective-permute-done | bytes 524320 | tf_op jit(solution)/shard_map/ppermute | solution.py:452
  75.8 0.7 slice_select_fusion.1
  76.5 1.4 all-to-all-done.1
  77.9 0.7 collective-permute-start.1
  78.6 2.8 %place_rows.6 = (bf16[256,512]{1,0:T(8,128)(2,1)S(1)}, bf16[256,512]{1,0:T(8,128)(2,1)S(1)}) custom-call(s32[32]{0:T(128)S(1)} %pad_add_fusion.info_ref, s32[1,2048]{1,0:T(1,128)S(1)} %bitcast.14, bf16[2048,512]{1,0:T(8,128)(2,1)} %bitcast.4.rows_ref), custom_call_target="tpu_custom_call" | custom-call | flops 1073741824 | bytes 2621440 | tf_op jit(solution)/shard_map/place_rows/pallas_call | solution.py:159
  81.4 0.0 copy-start.1
  81.5 3.4 %place_rows.7 = (bf16[256,512]{1,0:T(8,128)(2,1)S(1)}, bf16[512,512]{1,0:T(8,128)(2,1)S(1)}) custom-call(s32[32]{0:T(128)S(1)} %pad_add_fusion.info_ref, s32[1,2048]{1,0:T(1,128)S(1)} %bitcast.15, bf16[2048,512]{1,0:T(8,128)(2,1)} %bitcast.4.rows_ref), custom_call_target="tpu_custom_call" | custom-call | flops 1610612736 | bytes 2883584 | tf_op jit(solution)/shard_map/place_rows/pallas_call | solution.py:159
  84.9 0.0 collective-permute-done.2.refs_3_
  84.9 0.0 collective-permute-done.3.refs_4_
  84.9 0.0 collective-permute-done.1.refs_0_
  84.9 4.6 %collective-permute-start.4 = (bf16[512,512]{1,0:T(8,128)(2,1)S(1)}, bf16[512,512]{1,0:T(8,128)(2,1)S(1)}, u32[]{:S(2)}, u32[]{:S(2)}) collective-permute-start(bf16[512,512]{1,0:T(8,128)(2,1)S(1)} %get-tuple-element.53.refs_6_), channel_id=1, source_target_pairs={{0,1},{1,0},{2,3},{3,2},{4,5},{5,4},{6,7},{7,6},{8,9},{9,8},{10,11... | collective-permute-start | bytes 1572872 | tf_op jit(solution)/shard_map/ppermute | solution.py:452
  89.5 0.1 collective-permute-start.8
  89.6 2.3 %collective-permute-start.9 = (bf16[256,512]{1,0:T(8,128)(2,1)S(1)}, bf16[256,512]{1,0:T(8,128)(2,1)S(1)}, u32[]{:S(2)}, u32[]{:S(2)}) collective-permute-start(bf16[256,512]{1,0:T(8,128)(2,1)S(1)} %get-tuple-element.62), channel_id=1, source_target_pairs={{0,3},{1,2},{2,1},{3,0},{4,7},{5,6},{6,5},{7,4},{8,11},{9,10},{10,... | collective-permute-start | bytes 786440 | tf_op jit(solution)/shard_map/ppermute | solution.py:452
  91.8 15.0 %collective-permute-done.4.refs_7_ = bf16[512,512]{1,0:T(8,128)(2,1)S(1)} collective-permute-done((bf16[512,512]{1,0:T(8,128)(2,1)S(1)}, bf16[512,512]{1,0:T(8,128)(2,1)S(1)}, u32[]{:S(2)}, u32[]{:S(2)}) %collective-permute-start.4) | collective-permute-done | bytes 524320 | tf_op jit(solution)/shard_map/ppermute | solution.py:452
  106.8 0.7 collective-permute-start.5
  107.5 0.7 collective-permute-start.7
  108.2 0.7 collective-permute-start.6
  108.9 0.0 collective-permute-done.8.refs_8_
  108.9 4.5 %collective-permute-done.9.refs_9_ = bf16[256,512]{1,0:T(8,128)(2,1)S(1)} collective-permute-done((bf16[256,512]{1,0:T(8,128)(2,1)S(1)}, bf16[256,512]{1,0:T(8,128)(2,1)S(1)}, u32[]{:S(2)}, u32[]{:S(2)}) %collective-permute-start.9) | collective-permute-done | bytes 262176 | tf_op jit(solution)/shard_map/ppermute | solution.py:452
  113.4 0.0 copy-done.1
  113.4 5.4 %start_cluster.1 = (bf16[2048,1024]{1,0:T(8,128)(2,1)S(1)}, f32[2048,128]{1,0:T(8,128)S(1)}, f32[8,2048]{1,0:T(8,128)S(1)}, f32[8,1024]{1,0:T(8,128)S(1)}) custom-call(s32[32]{0:T(128)S(1)} %pad_add_fusion.info_ref, s32[2,40]{1,0:T(2,128)S(1)} %copy-done.1, bf16[256,512]{1,0:T(8,128)(2,1)S(1)} %get-tuple-element.56.refs_0_, ...), custom_call_target="tpu_custom_call" | custom-call | flops 4294967296 | bytes 4194304 | tf_op jit(solution)/shard_map/start_cluster/pallas_call | solution.py:378
  118.8 0.0 collective-permute-done.5.refs_1_
  118.8 0.0 collective-permute-done.7.refs_3_
  118.8 0.0 collective-permute-done.6.refs_2_
  118.8 0.0 copy-done
  118.8 2.3 %score_cluster.1 = (f32[4,12,128]{2,1,0:T(8,128)S(1)}, bf16[2048,1024]{1,0:T(8,128)(2,1)S(1)}, f32[2048,128]{1,0:T(8,128)S(1)}, f32[8,2048]{1,0:T(8,128)S(1)}, f32[8,1024]{1,0:T(8,128)S(1)}) custom-call(s32[32]{0:T(128)S(1)} %pad_add_fusion.info_ref, s32[2,40]{1,0:T(2,128)S(1)} %copy-done.1, ...), custom_call_target="tpu_custom_call", output_to_operand_aliasing={{1}: (6, {}), {2}: (7, {}), {3}: (8, {}), {4}: (9, {})} | custom-call | flops 1073741824 | bytes 4194304 | tf_op jit(solution)/shard_map/score_cluster/pallas_call | solution.py:407
  121.2 17.5 %all_to_all.24.back_ref = f32[4,12,128]{2,1,0:T(8,128)} all-to-all(f32[4,12,128]{2,1,0:T(8,128)S(1)} %get-tuple-element.67), channel_id=1, replica_groups=mesh['rows'=8,'own'=4] {'own'}, dimensions={0} | all-to-all | bytes 49152 | tf_op jit(solution)/shard_map/all_to_all | solution.py:524
  138.6 1.4 finish.1
  (6 shorter events, 0.1 us)
Async XLA Ops:
  2.0 14.6 %all-to-all-start = ((s32[32,1,256]{2,1,0:T(1,128)}), s32[32,1,256]{2,1,0:T(1,128)S(1)}, u32[]{:S(2)}, u32[]{:S(2)}) async-start(s32[32,1,256]{2,1,0:T(1,128)} %all_to_all.15), calls=%async_computation | async-start | bytes 65536 | tf_op jit(solution)/shard_map/all_to_all | solution.py:475
  16.6 5.0 %copy-start.2 = (s32[4]{0:T(128)S(1)}, s32[4]{0:T(128)}, u32[]{:S(2)}) copy-start(s32[4]{0:T(128)} %constant.64.clone) | copy-start | bytes 52
  16.6 30.3 %all-to-all-start.2 = ((bf16[8,256,512]{2,1,0:T(8,128)(2,1)}), bf16[8,256,512]{2,1,0:T(8,128)(2,1)S(1)}, u32[]{:S(2)}, u32[]{:S(2)}) async-start(bf16[8,256,512]{2,1,0:T(8,128)(2,1)} %bitcast.16), calls=%async_computation.2 | async-start | bytes 4194304 | tf_op jit(solution)/shard_map/all_to_all | solution.py:501
  23.7 95.1 %copy-start = (s32[32]{0:T(128)}, s32[32]{0:T(128)S(1)}, u32[]{:S(2)}) copy-start(s32[32]{0:T(128)S(1)} %pad_add_fusion.info_ref) | copy-start | bytes 388
  46.9 31.0 %all-to-all-start.1 = ((bf16[8,256,512]{2,1,0:T(8,128)(2,1)}), bf16[8,256,512]{2,1,0:T(8,128)(2,1)}, u32[]{:S(2)}, u32[]{:S(2)}) async-start(bf16[8,256,512]{2,1,0:T(8,128)(2,1)} %bitcast.17), calls=%async_computation.1 | async-start | bytes 4194304 | tf_op jit(solution)/shard_map/all_to_all | solution.py:501
  55.4 20.4 %collective-permute-start = (bf16[512,512]{1,0:T(8,128)(2,1)S(1)}, bf16[512,512]{1,0:T(8,128)(2,1)S(1)}, u32[]{:S(2)}, u32[]{:S(2)}) collective-permute-start(bf16[512,512]{1,0:T(8,128)(2,1)S(1)} %get-tuple-element.52.refs_1_), channel_id=1, source_target_pairs={{0,1},{1,0},{2,3},{3,2},{4,5},{5,4},{6,7},{7,6},{8,9},{9,8},{10,11... | collective-permute-start | bytes 1572872 | tf_op jit(solution)/shard_map/ppermute | solution.py:452
  57.1 27.7 %collective-permute-start.2 = (bf16[256,512]{1,0:T(8,128)(2,1)S(1)}, bf16[256,512]{1,0:T(8,128)(2,1)S(1)}, u32[]{:S(2)}, u32[]{:S(2)}) collective-permute-start(bf16[256,512]{1,0:T(8,128)(2,1)S(1)} %get-tuple-element.49), channel_id=1, source_target_pairs={{0,2},{1,3},{2,0},{3,1},{4,6},{5,7},{6,4},{7,5},{8,10},{9,11},{10,... | collective-permute-start | bytes 786440 | tf_op jit(solution)/shard_map/ppermute | solution.py:452
  58.8 26.0 %collective-permute-start.3 = (bf16[256,512]{1,0:T(8,128)(2,1)S(1)}, bf16[256,512]{1,0:T(8,128)(2,1)S(1)}, u32[]{:S(2)}, u32[]{:S(2)}) collective-permute-start(bf16[256,512]{1,0:T(8,128)(2,1)S(1)} %get-tuple-element.50), channel_id=1, source_target_pairs={{0,3},{1,2},{2,1},{3,0},{4,7},{5,6},{6,5},{7,4},{8,11},{9,10},{10,... | collective-permute-start | bytes 786440 | tf_op jit(solution)/shard_map/ppermute | solution.py:452
  77.9 7.0 %collective-permute-start.1 = (bf16[256,512]{1,0:T(8,128)(2,1)}, bf16[256,512]{1,0:T(8,128)(2,1)S(1)}, u32[]{:S(2)}, u32[]{:S(2)}) collective-permute-start(bf16[256,512]{1,0:T(8,128)(2,1)} %slice_select_fusion.1), channel_id=1, source_target_pairs={{1,2},{2,1},{5,6},{6,5},{9,10},{10,9},{13,14},{14,13},{17,18},{18,... | collective-permute-start | bytes 786440 | tf_op jit(solution)/shard_map/ppermute | solution.py:456
  81.4 32.0 %copy-start.1 = (s32[2,40]{1,0:T(2,128)S(1)}, s32[2,40]{1,0:T(2,128)}, u32[]{:S(2)}) copy-start(s32[2,40]{1,0:T(2,128)} %constant.66.clone.pairs_ref) | copy-start | bytes 964
  84.9 21.9 %collective-permute-start.4 = (bf16[512,512]{1,0:T(8,128)(2,1)S(1)}, bf16[512,512]{1,0:T(8,128)(2,1)S(1)}, u32[]{:S(2)}, u32[]{:S(2)}) collective-permute-start(bf16[512,512]{1,0:T(8,128)(2,1)S(1)} %get-tuple-element.53.refs_6_), channel_id=1, source_target_pairs={{0,1},{1,0},{2,3},{3,2},{4,5},{5,4},{6,7},{7,6},{8,9},{9,8},{10,11... | collective-permute-start | bytes 1572872 | tf_op jit(solution)/shard_map/ppermute | solution.py:452
  89.5 19.4 %collective-permute-start.8 = (bf16[256,512]{1,0:T(8,128)(2,1)S(1)}, bf16[256,512]{1,0:T(8,128)(2,1)S(1)}, u32[]{:S(2)}, u32[]{:S(2)}) collective-permute-start(bf16[256,512]{1,0:T(8,128)(2,1)S(1)} %get-tuple-element.61), channel_id=1, source_target_pairs={{0,2},{1,3},{2,0},{3,1},{4,6},{5,7},{6,4},{7,5},{8,10},{9,11},{10,... | collective-permute-start | bytes 786440 | tf_op jit(solution)/shard_map/ppermute | solution.py:452
  89.6 23.8 %collective-permute-start.9 = (bf16[256,512]{1,0:T(8,128)(2,1)S(1)}, bf16[256,512]{1,0:T(8,128)(2,1)S(1)}, u32[]{:S(2)}, u32[]{:S(2)}) collective-permute-start(bf16[256,512]{1,0:T(8,128)(2,1)S(1)} %get-tuple-element.62), channel_id=1, source_target_pairs={{0,3},{1,2},{2,1},{3,0},{4,7},{5,6},{6,5},{7,4},{8,11},{9,10},{10,... | collective-permute-start | bytes 786440 | tf_op jit(solution)/shard_map/ppermute | solution.py:452
  106.8 12.0 %collective-permute-start.5 = (bf16[256,512]{1,0:T(8,128)(2,1)S(1)}, bf16[256,512]{1,0:T(8,128)(2,1)S(1)}, u32[]{:S(2)}, u32[]{:S(2)}) collective-permute-start(bf16[256,512]{1,0:T(8,128)(2,1)S(1)} %slice.23), channel_id=1, source_target_pairs={{2,1},{5,6},{10,9},{13,14},{18,17},{21,22},{26,25},{29,30}} | collective-permute-start | bytes 786440 | tf_op jit(solution)/shard_map/ppermute | solution.py:462
  107.5 11.3 %collective-permute-start.7 = (bf16[256,512]{1,0:T(8,128)(2,1)S(1)}, bf16[256,512]{1,0:T(8,128)(2,1)S(1)}, u32[]{:S(2)}, u32[]{:S(2)}) collective-permute-start(bf16[256,512]{1,0:T(8,128)(2,1)S(1)} %get-tuple-element.55), channel_id=1, source_target_pairs={{2,1},{5,6},{10,9},{13,14},{18,17},{21,22},{26,25},{29,30}} | collective-permute-start | bytes 786440 | tf_op jit(solution)/shard_map/ppermute | solution.py:462
  108.2 10.6 %collective-permute-start.6 = (bf16[256,512]{1,0:T(8,128)(2,1)S(1)}, bf16[256,512]{1,0:T(8,128)(2,1)S(1)}, u32[]{:S(2)}, u32[]{:S(2)}) collective-permute-start(bf16[256,512]{1,0:T(8,128)(2,1)S(1)} %get-tuple-element.69), channel_id=1, source_target_pairs={{1,2},{2,1},{5,6},{6,5},{9,10},{10,9},{13,14},{14,13},{17,18},{18,... | collective-permute-start | bytes 786440 | tf_op jit(solution)/shard_map/ppermute | solution.py:456

commit v2 on v1

--- a/solution.py
+++ b/solution.py
@@ -62,9 +62,12 @@
             best = None
             for home in itertools.permutations(range(4)):
                 found = routes(biggest, home, parity)
-                if found is not None and (best is None or len(found[1]) < len(best[1][1])):
-                    best = (home, found)
-            home, (step, extra) = best
+                if found is None:
+                    continue
+                cost = (len(found[1]), len(found[0]))
+                if best is None or cost < best[0]:
+                    best = (cost, home, found)
+            _, home, (step, extra) = best
             for z in range(4):
                 row = rows[(parity,) + biggest][z]
                 row[HOME : HOME + 4] = home
@@ -335,24 +338,19 @@
         jnp.where(row == 1, low.astype(jnp.float32), 0.0),
     ).astype(jnp.bfloat16)
     ones = jnp.ones((8, LANES), jnp.float32)
-    for b in range(unit_b.shape[0] // ROWS):
-        at = slice(b * ROWS, (b + 1) * ROWS)
-
-        @pl.when(b < count_blocks)
-        def _(at=at):
-            along = lax.dot_general(
-                split, unit_b[at, :], ACROSS, preferred_element_type=jnp.float32
-            )
-            toward = jnp.sum(along, axis=0, keepdims=True)
-            rows = lax.dot_general(
-                ones,
-                row_acc[at, :],
-                ACROSS,
-                precision=lax.Precision.HIGHEST,
-                preferred_element_type=jnp.float32,
-            )
-            total = rows[:1] + jnp.sum(col_acc[:, at], axis=0, keepdims=True)
-            score_ref[:, at] = jnp.log(total) / SHARPNESS - toward
+    along = lax.dot_general(
+        split, unit_b[...], ACROSS, preferred_element_type=jnp.float32
+    )
+    toward = jnp.sum(along, axis=0, keepdims=True)
+    rows = lax.dot_general(
+        ones,
+        row_acc[...],
+        ACROSS,
+        precision=lax.Precision.HIGHEST,
+        preferred_element_type=jnp.float32,
+    )
+    total = rows[:1] + jnp.sum(col_acc[...], axis=0, keepdims=True)
+    score_ref[...] = jnp.log(total) / SHARPNESS - toward
 
     for s in range(4):
         out_ref[s, : 2 * per_half, :] = jnp.zeros((2 * per_half, LANES), jnp.float32)
@@ -517,7 +515,7 @@
             jnp.where(info[KC * 4 + FORWARD] == 1, from_pair[half:], pair[half:])
         )
     steps.append(step_move(carried[-1]))
-    first = moved[-1][2]
+    first = carried[-1]
     extras = [extra_move(tie((m[1][half:], first))[0]) for m in moved]
     begun = start_cluster(info, moved)
     result = score_cluster(info, list(zip(steps, extras)), begun)

time: 141 us -> 141 us (level)
  transfers between devices with their start and end apart: 13 -> 13, of which waited for: 6 -> 6; matrix products, arithmetic and copies ran while one was open for 3% -> 3% of each run, Pallas kernels for 18% -> 19%
where the time goes in v2:
time: 141 us; the launch traced here: 140 us
  waiting for transfers between devices  55.8 us (40%)
  Pallas kernels  30.2 us (21%)
  starting transfers between devices  29.5 us (21%)
  blocking collectives  17 us (12%)
  local copies, waits for them, and re-layouts  2.79 us (2%)
  other arithmetic  2.61 us (2%)
  between operations  2.2 us (2%)
    ppermute x6, waiting for transfers between devices, swap(): return lax.ppermute(x, 'own', [(z, z ^ by) for z in range(4)])  34.1 us
    all_to_all x2, waiting for transfers between devices, on_device(): lax.all_to_all(outgoing[k], 'rows', split_axis=0, concat_axis=0, tiled=True)  19.5 us
    all_to_all x1, blocking collectives, on_device(): lax.all_to_all(result, 'own', split_axis=0, concat_axis=0, tiled=True)  17 us
    ppermute x6, starting transfers between devices, swap(): return lax.ppermute(x, 'own', [(z, z ^ by) for z in range(4)])  11.5 us
    pallas_call x4, Pallas kernels, place_rows(): pl.pallas_call(functools.partial(place_body, blocks, half), in_specs=[sme...  10.3 us
    pallas_call x2, Pallas kernels, gather_rows(): pl.pallas_call(functools.partial(gather_body, first), in_specs=[vmem, pl....  10.1 us
    all_to_all x2, starting transfers between devices, on_device(): lax.all_to_all(outgoing[k], 'rows', split_axis=0, concat_axis=0, tiled=True)  8.08 us
    all_to_all x1, starting transfers between devices, on_device(): lax.all_to_all(jnp.repeat(dest_offset[0], 4, axis=0), ('rows', 'own'), sp...  7.3 us
  transfers between devices with their start and end apart: 13, of which 6 were waited for; matrix products, arithmetic and copies ran while one was open for 3% of the time, Pallas kernels for 19%

profile of v2, /device:TPU:0, one launch (start us, length us, event | category | flops | bytes accessed | tf_op | source)
XLA Modules:
  0.0 140.1 jit_solution(5099264019922359348)
XLA Ops:
  0.6 0.7 broadcast_in_dim.4
  1.3 0.7 all_to_all.15
  2.0 7.3 %all-to-all-start = ((s32[32,1,256]{2,1,0:T(1,128)}), s32[32,1,256]{2,1,0:T(1,128)S(1)}, u32[]{:S(2)}, u32[]{:S(2)}) async-start(s32[32,1,256]{2,1,0:T(1,128)} %all_to_all.15), calls=%async_computation | async-start | bytes 65536 | tf_op jit(solution)/shard_map/all_to_all | solution.py:473
  9.3 5.1 %gather_rows.3 = bf16[2048,512]{1,0:T(8,128)(2,1)} custom-call(s32[8,256]{1,0:T(8,128)} %bitcast.19, bf16[1024,1024]{1,0:T(8,128)(2,1)} %emb_ref.3), custom_call_target="tpu_custom_call" | custom-call | flops 2147483648 | bytes 3145728 | tf_op jit(solution)/shard_map/gather_rows/pallas_call | solution.py:119
  14.4 2.2 %all-to-all-done = s32[32,1,256]{2,1,0:T(1,128)S(1)} async-done(((s32[32,1,256]{2,1,0:T(1,128)}), s32[32,1,256]{2,1,0:T(1,128)S(1)}, u32[]{:S(2)}, u32[]{:S(2)}) %all-to-all-start) | async-done | bytes 32800 | tf_op jit(solution)/shard_map/all_to_all | solution.py:473
  16.6 0.0 copy-start.2
  16.6 3.7 %all-to-all-start.2 = ((bf16[8,256,512]{2,1,0:T(8,128)(2,1)}), bf16[8,256,512]{2,1,0:T(8,128)(2,1)S(1)}, u32[]{:S(2)}, u32[]{:S(2)}) async-start(bf16[8,256,512]{2,1,0:T(8,128)(2,1)} %bitcast.16), calls=%async_computation.2 | async-start | bytes 4194304 | tf_op jit(solution)/shard_map/all_to_all | solution.py:499
  20.3 0.1 reduce.18
  20.5 0.4 convert_reduce_fusion
  20.9 0.1 reshape.97
  21.0 0.6 iota_reduce_fusion
  21.6 0.0 copy-done.2
  21.6 0.6 multiply_reduce_fusion
  22.9 0.7 dynamic-slice_bitcast_fusion
  23.6 0.1 pad_add_fusion.info_ref
  23.7 0.0 copy-start
  23.7 5.1 %gather_rows.2 = bf16[2048,512]{1,0:T(8,128)(2,1)} custom-call(s32[8,256]{1,0:T(8,128)} %bitcast.20, bf16[1024,1024]{1,0:T(8,128)(2,1)} %emb_ref.3), custom_call_target="tpu_custom_call" | custom-call | flops 2147483648 | bytes 3145728 | tf_op jit(solution)/shard_map/gather_rows/pallas_call | solution.py:119
  28.8 18.1 %all-to-all-done.2 = bf16[8,256,512]{2,1,0:T(8,128)(2,1)S(1)} async-done(((bf16[8,256,512]{2,1,0:T(8,128)(2,1)}), bf16[8,256,512]{2,1,0:T(8,128)(2,1)S(1)}, u32[]{:S(2)}, u32[]{:S(2)}) %all-to-all-start.2) | async-done | bytes 2097184 | tf_op jit(solution)/shard_map/all_to_all | solution.py:499
  46.9 4.3 %all-to-all-start.1 = ((bf16[8,256,512]{2,1,0:T(8,128)(2,1)}), bf16[8,256,512]{2,1,0:T(8,128)(2,1)}, u32[]{:S(2)}, u32[]{:S(2)}) async-start(bf16[8,256,512]{2,1,0:T(8,128)(2,1)} %bitcast.17), calls=%async_computation.1 | async-start | bytes 4194304 | tf_op jit(solution)/shard_map/all_to_all | solution.py:499
  51.3 1.8 %place_rows.4 = (bf16[256,512]{1,0:T(8,128)(2,1)S(1)}, bf16[256,512]{1,0:T(8,128)(2,1)S(1)}) custom-call(s32[32]{0:T(128)S(1)} %pad_add_fusion.info_ref, s32[1,2048]{1,0:T(1,128)S(1)} %bitcast.12, bf16[2048,512]{1,0:T(8,128)(2,1)S(1)} %bitcast.10), custom_call_target="tpu_custom_call" | custom-call | flops 1073741824 | bytes 2621440 | tf_op jit(solution)/shard_map/place_rows/pallas_call | solution.py:162
  53.1 2.3 %place_rows.5 = (bf16[256,512]{1,0:T(8,128)(2,1)S(1)}, bf16[512,512]{1,0:T(8,128)(2,1)S(1)}) custom-call(s32[32]{0:T(128)S(1)} %pad_add_fusion.info_ref, s32[1,2048]{1,0:T(1,128)S(1)} %bitcast.13, bf16[2048,512]{1,0:T(8,128)(2,1)S(1)} %bitcast.11), custom_call_target="tpu_custom_call" | custom-call | flops 1610612736 | bytes 2883584 | tf_op jit(solution)/shard_map/place_rows/pallas_call | solution.py:162
  55.4 0.5 collective-permute-start
  55.9 0.6 slice.20
  57.1 1.7 %collective-permute-start.2 = (bf16[256,512]{1,0:T(8,128)(2,1)S(1)}, bf16[256,512]{1,0:T(8,128)(2,1)S(1)}, u32[]{:S(2)}, u32[]{:S(2)}) collective-permute-start(bf16[256,512]{1,0:T(8,128)(2,1)S(1)} %get-tuple-element.49), channel_id=1, source_target_pairs={{0,2},{1,3},{2,0},{3,1},{4,6},{5,7},{6,4},{7,5},{8,10},{9,11},{10,... | collective-permute-start | bytes 786440 | tf_op jit(solution)/shard_map/ppermute | solution.py:450
  58.8 2.4 %collective-permute-start.3 = (bf16[256,512]{1,0:T(8,128)(2,1)S(1)}, bf16[256,512]{1,0:T(8,128)(2,1)S(1)}, u32[]{:S(2)}, u32[]{:S(2)}) collective-permute-start(bf16[256,512]{1,0:T(8,128)(2,1)S(1)} %get-tuple-element.50), channel_id=1, source_target_pairs={{0,3},{1,2},{2,1},{3,0},{4,7},{5,6},{6,5},{7,4},{8,11},{9,10},{10,... | collective-permute-start | bytes 786440 | tf_op jit(solution)/shard_map/ppermute | solution.py:450
  61.2 14.6 %collective-permute-done.refs_2_ = bf16[512,512]{1,0:T(8,128)(2,1)S(1)} collective-permute-done((bf16[512,512]{1,0:T(8,128)(2,1)S(1)}, bf16[512,512]{1,0:T(8,128)(2,1)S(1)}, u32[]{:S(2)}, u32[]{:S(2)}) %collective-permute-start) | collective-permute-done | bytes 524320 | tf_op jit(solution)/shard_map/ppermute | solution.py:450
  75.8 0.7 slice_select_fusion.1
  76.5 1.4 all-to-all-done.1
  77.9 0.7 collective-permute-start.1
  78.6 2.8 %place_rows.6 = (bf16[256,512]{1,0:T(8,128)(2,1)S(1)}, bf16[256,512]{1,0:T(8,128)(2,1)S(1)}) custom-call(s32[32]{0:T(128)S(1)} %pad_add_fusion.info_ref, s32[1,2048]{1,0:T(1,128)S(1)} %bitcast.14, bf16[2048,512]{1,0:T(8,128)(2,1)} %bitcast.4.rows_ref), custom_call_target="tpu_custom_call" | custom-call | flops 1073741824 | bytes 2621440 | tf_op jit(solution)/shard_map/place_rows/pallas_call | solution.py:162
  81.4 0.0 copy-start.1
  81.5 3.4 %place_rows.7 = (bf16[256,512]{1,0:T(8,128)(2,1)S(1)}, bf16[512,512]{1,0:T(8,128)(2,1)S(1)}) custom-call(s32[32]{0:T(128)S(1)} %pad_add_fusion.info_ref, s32[1,2048]{1,0:T(1,128)S(1)} %bitcast.15, bf16[2048,512]{1,0:T(8,128)(2,1)} %bitcast.4.rows_ref), custom_call_target="tpu_custom_call" | custom-call | flops 1610612736 | bytes 2883584 | tf_op jit(solution)/shard_map/place_rows/pallas_call | solution.py:162
  84.9 0.0 collective-permute-done.2.refs_3_
  84.9 0.0 collective-permute-done.3.refs_4_
  84.9 0.0 collective-permute-done.1.refs_0_
  84.9 4.6 %collective-permute-start.4 = (bf16[512,512]{1,0:T(8,128)(2,1)S(1)}, bf16[512,512]{1,0:T(8,128)(2,1)S(1)}, u32[]{:S(2)}, u32[]{:S(2)}) collective-permute-start(bf16[512,512]{1,0:T(8,128)(2,1)S(1)} %get-tuple-element.53.refs_6_), channel_id=1, source_target_pairs={{0,1},{1,0},{2,3},{3,2},{4,5},{5,4},{6,7},{7,6},{8,9},{9,8},{10,11... | collective-permute-start | bytes 1572872 | tf_op jit(solution)/shard_map/ppermute | solution.py:450
  89.5 0.1 collective-permute-start.8
  89.6 2.3 %collective-permute-start.9 = (bf16[256,512]{1,0:T(8,128)(2,1)S(1)}, bf16[256,512]{1,0:T(8,128)(2,1)S(1)}, u32[]{:S(2)}, u32[]{:S(2)}) collective-permute-start(bf16[256,512]{1,0:T(8,128)(2,1)S(1)} %get-tuple-element.62), channel_id=1, source_target_pairs={{0,3},{1,2},{2,1},{3,0},{4,7},{5,6},{6,5},{7,4},{8,11},{9,10},{10,... | collective-permute-start | bytes 786440 | tf_op jit(solution)/shard_map/ppermute | solution.py:450
  91.8 15.0 %collective-permute-done.4.refs_7_ = bf16[512,512]{1,0:T(8,128)(2,1)S(1)} collective-permute-done((bf16[512,512]{1,0:T(8,128)(2,1)S(1)}, bf16[512,512]{1,0:T(8,128)(2,1)S(1)}, u32[]{:S(2)}, u32[]{:S(2)}) %collective-permute-start.4) | collective-permute-done | bytes 524320 | tf_op jit(solution)/shard_map/ppermute | solution.py:450
  106.8 0.7 collective-permute-start.6
  107.5 0.7 collective-permute-start.5
  108.2 0.7 collective-permute-start.7
  108.9 0.0 collective-permute-done.8.refs_8_
  108.9 4.5 %collective-permute-done.9.refs_9_ = bf16[256,512]{1,0:T(8,128)(2,1)S(1)} collective-permute-done((bf16[256,512]{1,0:T(8,128)(2,1)S(1)}, bf16[256,512]{1,0:T(8,128)(2,1)S(1)}, u32[]{:S(2)}, u32[]{:S(2)}) %collective-permute-start.9) | collective-permute-done | bytes 262176 | tf_op jit(solution)/shard_map/ppermute | solution.py:450
  113.4 0.0 copy-done.1
  113.4 5.5 %start_cluster.1 = (bf16[2048,1024]{1,0:T(8,128)(2,1)S(1)}, f32[2048,128]{1,0:T(8,128)S(1)}, f32[8,2048]{1,0:T(8,128)S(1)}, f32[8,1024]{1,0:T(8,128)S(1)}) custom-call(s32[32]{0:T(128)S(1)} %pad_add_fusion.info_ref, s32[2,40]{1,0:T(2,128)S(1)} %copy-done.1, bf16[256,512]{1,0:T(8,128)(2,1)S(1)} %get-tuple-element.56.refs_0_, ...), custom_call_target="tpu_custom_call" | custom-call | flops 4294967296 | bytes 4194304 | tf_op jit(solution)/shard_map/start_cluster/pallas_call | solution.py:376
  118.9 0.0 collective-permute-done.5.refs_1_
  118.9 0.0 collective-permute-done.7.refs_3_
  119.0 0.0 collective-permute-done.6.refs_2_
  119.0 0.0 copy-done
  119.0 2.8 %score_cluster.1 = (f32[4,12,128]{2,1,0:T(8,128)S(1)}, bf16[2048,1024]{1,0:T(8,128)(2,1)S(1)}, f32[2048,128]{1,0:T(8,128)S(1)}, f32[8,2048]{1,0:T(8,128)S(1)}, f32[8,1024]{1,0:T(8,128)S(1)}) custom-call(s32[32]{0:T(128)S(1)} %pad_add_fusion.info_ref, s32[2,40]{1,0:T(2,128)S(1)} %copy-done.1, ...), custom_call_target="tpu_custom_call", output_to_operand_aliasing={{1}: (6, {}), {2}: (7, {}), {3}: (8, {}), {4}: (9, {})} | custom-call | flops 1073741824 | bytes 4194304 | tf_op jit(solution)/shard_map/score_cluster/pallas_call | solution.py:405
  121.8 17.0 %all_to_all.24.back_ref = f32[4,12,128]{2,1,0:T(8,128)} all-to-all(f32[4,12,128]{2,1,0:T(8,128)S(1)} %get-tuple-element.67), channel_id=1, replica_groups=mesh['rows'=8,'own'=4] {'own'}, dimensions={0} | all-to-all | bytes 49152 | tf_op jit(solution)/shard_map/all_to_all | solution.py:522
  138.7 1.4 finish.1
  (6 shorter events, 0.1 us)
Async XLA Ops:
  2.0 14.6 %all-to-all-start = ((s32[32,1,256]{2,1,0:T(1,128)}), s32[32,1,256]{2,1,0:T(1,128)S(1)}, u32[]{:S(2)}, u32[]{:S(2)}) async-start(s32[32,1,256]{2,1,0:T(1,128)} %all_to_all.15), calls=%async_computation | async-start | bytes 65536 | tf_op jit(solution)/shard_map/all_to_all | solution.py:473
  16.6 5.0 %copy-start.2 = (s32[4]{0:T(128)S(1)}, s32[4]{0:T(128)}, u32[]{:S(2)}) copy-start(s32[4]{0:T(128)} %constant.64.clone) | copy-start | bytes 52
  16.6 30.3 %all-to-all-start.2 = ((bf16[8,256,512]{2,1,0:T(8,128)(2,1)}), bf16[8,256,512]{2,1,0:T(8,128)(2,1)S(1)}, u32[]{:S(2)}, u32[]{:S(2)}) async-start(bf16[8,256,512]{2,1,0:T(8,128)(2,1)} %bitcast.16), calls=%async_computation.2 | async-start | bytes 4194304 | tf_op jit(solution)/shard_map/all_to_all | solution.py:499
  23.7 95.3 %copy-start = (s32[32]{0:T(128)}, s32[32]{0:T(128)S(1)}, u32[]{:S(2)}) copy-start(s32[32]{0:T(128)S(1)} %pad_add_fusion.info_ref) | copy-start | bytes 388
  46.9 31.0 %all-to-all-start.1 = ((bf16[8,256,512]{2,1,0:T(8,128)(2,1)}), bf16[8,256,512]{2,1,0:T(8,128)(2,1)}, u32[]{:S(2)}, u32[]{:S(2)}) async-start(bf16[8,256,512]{2,1,0:T(8,128)(2,1)} %bitcast.17), calls=%async_computation.1 | async-start | bytes 4194304 | tf_op jit(solution)/shard_map/all_to_all | solution.py:499
  55.4 20.4 %collective-permute-start = (bf16[512,512]{1,0:T(8,128)(2,1)S(1)}, bf16[512,512]{1,0:T(8,128)(2,1)S(1)}, u32[]{:S(2)}, u32[]{:S(2)}) collective-permute-start(bf16[512,512]{1,0:T(8,128)(2,1)S(1)} %get-tuple-element.52.refs_1_), channel_id=1, source_target_pairs={{0,1},{1,0},{2,3},{3,2},{4,5},{5,4},{6,7},{7,6},{8,9},{9,8},{10,11... | collective-permute-start | bytes 1572872 | tf_op jit(solution)/shard_map/ppermute | solution.py:450
  57.1 27.7 %collective-permute-start.2 = (bf16[256,512]{1,0:T(8,128)(2,1)S(1)}, bf16[256,512]{1,0:T(8,128)(2,1)S(1)}, u32[]{:S(2)}, u32[]{:S(2)}) collective-permute-start(bf16[256,512]{1,0:T(8,128)(2,1)S(1)} %get-tuple-element.49), channel_id=1, source_target_pairs={{0,2},{1,3},{2,0},{3,1},{4,6},{5,7},{6,4},{7,5},{8,10},{9,11},{10,... | collective-permute-start | bytes 786440 | tf_op jit(solution)/shard_map/ppermute | solution.py:450
  58.8 26.0 %collective-permute-start.3 = (bf16[256,512]{1,0:T(8,128)(2,1)S(1)}, bf16[256,512]{1,0:T(8,128)(2,1)S(1)}, u32[]{:S(2)}, u32[]{:S(2)}) collective-permute-start(bf16[256,512]{1,0:T(8,128)(2,1)S(1)} %get-tuple-element.50), channel_id=1, source_target_pairs={{0,3},{1,2},{2,1},{3,0},{4,7},{5,6},{6,5},{7,4},{8,11},{9,10},{10,... | collective-permute-start | bytes 786440 | tf_op jit(solution)/shard_map/ppermute | solution.py:450
  77.9 7.0 %collective-permute-start.1 = (bf16[256,512]{1,0:T(8,128)(2,1)}, bf16[256,512]{1,0:T(8,128)(2,1)S(1)}, u32[]{:S(2)}, u32[]{:S(2)}) collective-permute-start(bf16[256,512]{1,0:T(8,128)(2,1)} %slice_select_fusion.1), channel_id=1, source_target_pairs={{1,2},{2,1},{5,6},{6,5},{9,10},{10,9},{13,14},{14,13},{17,18},{18,... | collective-permute-start | bytes 786440 | tf_op jit(solution)/shard_map/ppermute | solution.py:454
  81.4 32.0 %copy-start.1 = (s32[2,40]{1,0:T(2,128)S(1)}, s32[2,40]{1,0:T(2,128)}, u32[]{:S(2)}) copy-start(s32[2,40]{1,0:T(2,128)} %constant.66.clone.pairs_ref) | copy-start | bytes 964
  84.9 21.9 %collective-permute-start.4 = (bf16[512,512]{1,0:T(8,128)(2,1)S(1)}, bf16[512,512]{1,0:T(8,128)(2,1)S(1)}, u32[]{:S(2)}, u32[]{:S(2)}) collective-permute-start(bf16[512,512]{1,0:T(8,128)(2,1)S(1)} %get-tuple-element.53.refs_6_), channel_id=1, source_target_pairs={{0,1},{1,0},{2,3},{3,2},{4,5},{5,4},{6,7},{7,6},{8,9},{9,8},{10,11... | collective-permute-start | bytes 1572872 | tf_op jit(solution)/shard_map/ppermute | solution.py:450
  89.5 19.4 %collective-permute-start.8 = (bf16[256,512]{1,0:T(8,128)(2,1)S(1)}, bf16[256,512]{1,0:T(8,128)(2,1)S(1)}, u32[]{:S(2)}, u32[]{:S(2)}) collective-permute-start(bf16[256,512]{1,0:T(8,128)(2,1)S(1)} %get-tuple-element.61), channel_id=1, source_target_pairs={{0,2},{1,3},{2,0},{3,1},{4,6},{5,7},{6,4},{7,5},{8,10},{9,11},{10,... | collective-permute-start | bytes 786440 | tf_op jit(solution)/shard_map/ppermute | solution.py:450
  89.6 23.8 %collective-permute-start.9 = (bf16[256,512]{1,0:T(8,128)(2,1)S(1)}, bf16[256,512]{1,0:T(8,128)(2,1)S(1)}, u32[]{:S(2)}, u32[]{:S(2)}) collective-permute-start(bf16[256,512]{1,0:T(8,128)(2,1)S(1)} %get-tuple-element.62), channel_id=1, source_target_pairs={{0,3},{1,2},{2,1},{3,0},{4,7},{5,6},{6,5},{7,4},{8,11},{9,10},{10,... | collective-permute-start | bytes 786440 | tf_op jit(solution)/shard_map/ppermute | solution.py:450
  106.8 12.1 %collective-permute-start.6 = (bf16[256,512]{1,0:T(8,128)(2,1)S(1)}, bf16[256,512]{1,0:T(8,128)(2,1)S(1)}, u32[]{:S(2)}, u32[]{:S(2)}) collective-permute-start(bf16[256,512]{1,0:T(8,128)(2,1)S(1)} %get-tuple-element.69), channel_id=1, source_target_pairs={{1,2},{2,1},{5,6},{6,5},{9,10},{10,9},{13,14},{14,13},{17,18},{18,... | collective-permute-start | bytes 786440 | tf_op jit(solution)/shard_map/ppermute | solution.py:454
  107.5 11.4 %collective-permute-start.5 = (bf16[256,512]{1,0:T(8,128)(2,1)S(1)}, bf16[256,512]{1,0:T(8,128)(2,1)S(1)}, u32[]{:S(2)}, u32[]{:S(2)}) collective-permute-start(bf16[256,512]{1,0:T(8,128)(2,1)S(1)} %slice.23), channel_id=1, source_target_pairs={{2,1},{5,6},{10,9},{13,14},{18,17},{21,22},{26,25},{29,30}} | collective-permute-start | bytes 786440 | tf_op jit(solution)/shard_map/ppermute | solution.py:460
  108.2 10.7 %collective-permute-start.7 = (bf16[256,512]{1,0:T(8,128)(2,1)S(1)}, bf16[256,512]{1,0:T(8,128)(2,1)S(1)}, u32[]{:S(2)}, u32[]{:S(2)}) collective-permute-start(bf16[256,512]{1,0:T(8,128)(2,1)S(1)} %get-tuple-element.55), channel_id=1, source_target_pairs={{2,1},{5,6},{10,9},{13,14},{18,17},{21,22},{26,25},{29,30}} | collective-permute-start | bytes 786440 | tf_op jit(solution)/shard_map/ppermute | solution.py:460
